TPU v7x, 128 devices: a whole 4x4x4 slice. The times are simulated.
128 devices in a mesh: patch: 16 (over y, x), col: 8 (over z, core).
Axes of the slice: x: 4, y: 4, z: 4, core: 2. Of those that a mesh axis runs over, the one named last changes fastest.
Arguments:
- potential0: float32 [512, 16, 128], P(('patch', 'col')), may hold values from -3 to 3
- source_term: float32 [512, 16, 128], P(('patch', 'col')), may hold values from -9 to 9
- self_coef: float32 [512, 128], P(('patch', 'col')), may hold values from 1 to 4
- nearfield: float32 [512, 24, 128, 128], P(('patch', 'col')), may hold values from -0.109375 to 0.109375
- precond: float32 [512, 128, 128], P(('patch', 'col')), may hold values from -1 to 2
- exch_current: float32 [512, 128], P(('patch', 'col')), may hold values from 0.05 to 0.5
- conductance: float32 [512, 128], P(('patch', 'col')), may hold values from 0.1 to 1
- member: int32 [512, 128], P(('patch', 'col')), may hold values from 0 to 63
- anode_drive: float32 [64], replicated, may hold values from -1 to 1
- pair_source: int32 [512, 24], P(('patch', 'col')), may hold values from 0 to 39
- pair_count: int32 [512], P(('patch', 'col')), may hold values from 1 to 24, as said below
Outputs:
- potential: float32 [512, 16, 128], P(('patch', 'col'))
- residual: float32 [512, 16, 128], P(('patch', 'col'))
Inputs may be any that keep to these rules, and one draw needn't show every extreme that they name: Slots k < pair_count[b] of block b are live; some block has all 24 slots live, and the blocks of some devices hold far more live pairs than those of others.
All inputs are finite; a program needn't handle non-finite values.
Results may differ from a plain program's by a relative error of at most 0.0003.
Values sent between devices are 32-bit elements; how exact they have to be, the bound alone decides.
A program may use at most 64 MiB of HBM per device.

v0:
```python
import jax
import jax.numpy as jnp
from jax import lax
from jax.sharding import PartitionSpec as P

NEWTON = 2
GMRES = 2
ALPHA = 0.6
BETA = 0.4
EPS = 1e-06


def from_behind(array, axis, by):
    size = lax.axis_size(axis)
    return lax.ppermute(array, axis, [(i, (i + by) % size) for i in range(size)])


def column_sum(left, right):
    return jnp.sum(left * right, axis=(0, 2))


def least_squares(columns, beta):
    depth = len(columns)
    hessen = jnp.zeros((beta.shape[0], depth + 1, depth), jnp.float32)
    for place in range(depth):
        hessen = hessen.at[:, : place + 2, place].set(columns[place].T)
    gram = jnp.einsum("cij,cik->cjk", hessen, hessen, precision=lax.Precision.HIGHEST)
    right = beta[:, None] * hessen[:, 0, :]
    lower = jnp.linalg.cholesky(gram)
    middle = jax.scipy.linalg.solve_triangular(lower, right[:, :, None], lower=True)
    return jax.scipy.linalg.solve_triangular(lower, middle, lower=True, trans=1)[:, :, 0]


def body(
    potential0,
    source_term,
    self_coef,
    nearfield,
    precond,
    exch_current,
    conductance,
    member,
    anode_drive,
    pair_source,
    pair_count,
):
    pair_slots = pair_source.shape[1]
    live_mask = (jnp.arange(pair_slots, dtype=jnp.int32)[None, :] < pair_count[:, None]).astype(
        jnp.float32
    )
    members = anode_drive.shape[0]
    onehot = (jnp.arange(members, dtype=jnp.int32)[:, None, None] == member[None]).astype(
        jnp.float32
    )
    member_drive = jnp.sum(onehot * anode_drive[:, None, None], axis=0)
    diagonal = self_coef[:, None, :]
    current = exch_current[:, None, :]
    conduct = conductance[:, None, :]

    def near_field(field):
        own_patch = lax.all_gather(field, "col", axis=0, tiled=True)
        before = from_behind(field, "patch", 1)
        following = from_behind(field, "patch", -1)
        stacked = jnp.concatenate([own_patch, before, following], axis=0)
        sources = stacked[pair_source]
        return jnp.einsum(
            "bkij,bkcj->bci",
            nearfield,
            sources * live_mask[:, :, None, None],
            precision=lax.Precision.HIGHEST,
        )

    def mismatch(field, near_value):
        grow = jnp.exp(ALPHA * field)
        shrink = jnp.exp(-BETA * field)
        value = (
            diagonal * field
            + near_value
            + current * (grow - shrink)
            + conduct * (field - member_drive[:, None, :])
            - source_term
        )
        slope = current * (ALPHA * grow + BETA * shrink) + conduct
        return (value, slope)

    field = potential0
    near_now = near_field(field)
    for newton in range(NEWTON):
        value, slope = mismatch(field, near_now)
        start = -value
        beta = jnp.sqrt(lax.psum(column_sum(start, start), ("patch", "col")) + EPS)
        basis = [start / beta[None, :, None]]
        directions = []
        near_images = []
        columns = []
        for step in range(GMRES):
            direction = jnp.einsum(
                "bij,bcj->bci", precond, basis[step], precision=lax.Precision.HIGHEST
            )
            directions.append(direction)
            near_image = near_field(direction)
            near_images.append(near_image)
            image = diagonal * direction + near_image + slope * direction
            coeffs = []
            for place in range(step + 1):
                coeff = lax.psum(column_sum(basis[place], image), ("patch", "col"))
                image = image - coeff[None, :, None] * basis[place]
                coeffs.append(coeff)
            norm = jnp.sqrt(lax.psum(column_sum(image, image), ("patch", "col")) + EPS)
            basis.append(image / norm[None, :, None])
            columns.append(jnp.stack(coeffs + [norm]))
        weights = least_squares(columns, beta)
        update = jnp.zeros_like(field)
        for step in range(GMRES):
            update = update + weights[:, step][None, :, None] * directions[step]
        field = field + update
        near_now = near_field(field)
    final_value, final_slope = mismatch(field, near_now)
    return (field, final_value)


def solution(mesh):
    return jax.shard_map(
        body,
        mesh=mesh,
        in_specs=(
            P(("patch", "col"), None, None),
            P(("patch", "col"), None, None),
            P(("patch", "col"), None),
            P(("patch", "col"), None, None, None),
            P(("patch", "col"), None, None),
            P(("patch", "col"), None),
            P(("patch", "col"), None),
            P(("patch", "col"), None),
            P(),
            P(("patch", "col"), None),
            P(("patch", "col")),
        ),
        out_specs=(P(("patch", "col"), None, None), P(("patch", "col"), None, None)),
        check_vma=False,
    )
```

profile of v0, /device:TPU:1, one launch (start us, length us, event | category | flops | bytes accessed | tf_op | source)
XLA Modules:
  0.0 974.0 jit_solution(4111155873102971596)
XLA Ops:
  0.7 2.1 collective-permute-start
  2.8 3.8 collective-permute-start.1
  6.6 15.1 %all_gather.21 = f32[32,16,128]{2,1,0:T(8,128)S(1)} all-gather(f32[4,16,128]{2,1,0:T(8,128)} %param.24), channel_id=1, replica_groups=mesh['patch'=16,'col'=8] {'col'}, dimensions={0}, use_global_device_ids=true | all-gather | bytes 294912 | tf_op jit(solution)/shard_map/all_gather | solution.py:61
  22.5 0.7 fusion.40
  23.2 0.8 select_reduce_fusion
  24.0 0.7 gather_fusion
  24.7 7.6 multiply_reduce_fusion.11
  32.3 64.2 %psum.84 = f32[16]{0:T(128)S(1)} all-reduce(f32[16]{0:T(128)S(1)} %get-tuple-element.61), channel_id=1, replica_groups=mesh['patch'=16,'col'=8] {'patch','col'}, use_global_device_ids=true, to_apply=%region_2.0 | all-reduce | flops 16 | bytes 128 | tf_op jit(solution)/shard_map/psum | solution.py:91
  97.3 4.6 collective-permute-start.3
  101.9 13.9 %all_gather.22 = f32[32,16,128]{2,1,0:T(8,128)S(1)} all-gather(f32[4,16,128]{2,1,0:T(8,128)S(1)} %fusion.43), channel_id=1, replica_groups=mesh['patch'=16,'col'=8] {'col'}, dimensions={0}, use_global_device_ids=true | all-gather | bytes 294912 | tf_op jit(solution)/shard_map/all_gather | solution.py:61
  115.8 0.7 gather_fusion.1
  116.5 7.5 multiply_reduce_fusion.10
  124.0 63.4 %psum.85 = f32[16]{0:T(128)S(1)} all-reduce(f32[16]{0:T(128)S(1)} %get-tuple-element.63), channel_id=1, replica_groups=mesh['patch'=16,'col'=8] {'patch','col'}, use_global_device_ids=true, to_apply=%region_4.0 | all-reduce | flops 16 | bytes 128 | tf_op jit(solution)/shard_map/psum | solution.py:106
  187.6 63.0 %psum.86 = f32[16]{0:T(128)S(1)} all-reduce(f32[16]{0:T(128)S(1)} %multiply_reduce_fusion.9), channel_id=1, replica_groups=mesh['patch'=16,'col'=8] {'patch','col'}, use_global_device_ids=true, to_apply=%region_6.0 | all-reduce | flops 16 | bytes 128 | tf_op jit(solution)/shard_map/psum | solution.py:109
  251.2 0.8 collective-permute-start.4
  252.1 4.0 collective-permute-start.5
  256.0 13.8 %all_gather.23 = f32[32,16,128]{2,1,0:T(8,128)S(1)} all-gather(f32[4,16,128]{2,1,0:T(8,128)S(1)} %fusion.44), channel_id=1, replica_groups=mesh['patch'=16,'col'=8] {'col'}, dimensions={0}, use_global_device_ids=true | all-gather | bytes 294912 | tf_op jit(solution)/shard_map/all_gather | solution.py:61
  269.8 0.7 gather_fusion.2
  270.5 7.5 multiply_reduce_fusion.8
  278.0 64.4 %psum.87 = f32[16]{0:T(128)S(1)} all-reduce(f32[16]{0:T(128)S(1)} %get-tuple-element.65), channel_id=1, replica_groups=mesh['patch'=16,'col'=8] {'patch','col'}, use_global_device_ids=true, to_apply=%region_8.0 | all-reduce | flops 16 | bytes 128 | tf_op jit(solution)/shard_map/psum | solution.py:106
  342.6 62.5 %psum.88 = f32[16]{0:T(128)S(1)} all-reduce(f32[16]{0:T(128)S(1)} %multiply_reduce_fusion.7), channel_id=1, replica_groups=mesh['patch'=16,'col'=8] {'patch','col'}, use_global_device_ids=true, to_apply=%region_10.0 | all-reduce | flops 16 | bytes 128 | tf_op jit(solution)/shard_map/psum | solution.py:106
  405.3 64.0 %psum.89 = f32[16]{0:T(128)S(1)} all-reduce(f32[16]{0:T(128)S(1)} %multiply_reduce_fusion.6), channel_id=1, replica_groups=mesh['patch'=16,'col'=8] {'patch','col'}, use_global_device_ids=true, to_apply=%region_12.0 | all-reduce | flops 16 | bytes 128 | tf_op jit(solution)/shard_map/psum | solution.py:109
  470.0 3.1 custom-call.12
  473.3 3.0 custom-call.14
  476.7 4.8 collective-permute-start.7
  481.5 14.5 %all_gather.24 = f32[32,16,128]{2,1,0:T(8,128)S(1)} all-gather(f32[4,16,128]{2,1,0:T(8,128)S(1)} %add_add_fusion.1), channel_id=1, replica_groups=mesh['patch'=16,'col'=8] {'col'}, dimensions={0}, use_global_device_ids=true | all-gather | bytes 294912 | tf_op jit(solution)/shard_map/all_gather | solution.py:61
  496.7 7.5 multiply_reduce_fusion.5
  504.2 61.8 %psum.90 = f32[16]{0:T(128)S(1)} all-reduce(f32[16]{0:T(128)S(1)} %get-tuple-element.67), channel_id=1, replica_groups=mesh['patch'=16,'col'=8] {'patch','col'}, use_global_device_ids=true, to_apply=%region_16.0 | all-reduce | flops 16 | bytes 128 | tf_op jit(solution)/shard_map/psum | solution.py:91
  566.6 1.2 collective-permute-start.8
  567.7 3.7 collective-permute-start.9
  571.4 13.9 %all_gather.25 = f32[32,16,128]{2,1,0:T(8,128)S(1)} all-gather(f32[4,16,128]{2,1,0:T(8,128)S(1)} %fusion.45), channel_id=1, replica_groups=mesh['patch'=16,'col'=8] {'col'}, dimensions={0}, use_global_device_ids=true | all-gather | bytes 294912 | tf_op jit(solution)/shard_map/all_gather | solution.py:61
  585.3 0.7 gather_fusion.4
  586.0 7.5 multiply_reduce_fusion.4
  593.5 63.5 %psum.91 = f32[16]{0:T(128)S(1)} all-reduce(f32[16]{0:T(128)S(1)} %get-tuple-element.69), channel_id=1, replica_groups=mesh['patch'=16,'col'=8] {'patch','col'}, use_global_device_ids=true, to_apply=%region_18.0 | all-reduce | flops 16 | bytes 128 | tf_op jit(solution)/shard_map/psum | solution.py:106
  657.1 62.6 %psum.92 = f32[16]{0:T(128)S(1)} all-reduce(f32[16]{0:T(128)S(1)} %multiply_reduce_fusion.3), channel_id=1, replica_groups=mesh['patch'=16,'col'=8] {'patch','col'}, use_global_device_ids=true, to_apply=%region_20.0 | all-reduce | flops 16 | bytes 128 | tf_op jit(solution)/shard_map/psum | solution.py:109
  720.2 0.8 collective-permute-start.10
  721.1 4.0 collective-permute-start.11
  725.0 14.0 %all_gather.26 = f32[32,16,128]{2,1,0:T(8,128)S(1)} all-gather(f32[4,16,128]{2,1,0:T(8,128)S(1)} %fusion.46), channel_id=1, replica_groups=mesh['patch'=16,'col'=8] {'col'}, dimensions={0}, use_global_device_ids=true | all-gather | bytes 294912 | tf_op jit(solution)/shard_map/all_gather | solution.py:61
  739.1 0.7 gather_fusion.5
  739.8 7.5 multiply_reduce_fusion.2
  747.2 64.4 %psum.93 = f32[16]{0:T(128)S(1)} all-reduce(f32[16]{0:T(128)S(1)} %get-tuple-element.71), channel_id=1, replica_groups=mesh['patch'=16,'col'=8] {'patch','col'}, use_global_device_ids=true, to_apply=%region_22.0 | all-reduce | flops 16 | bytes 128 | tf_op jit(solution)/shard_map/psum | solution.py:106
  811.8 62.5 %psum.94 = f32[16]{0:T(128)S(1)} all-reduce(f32[16]{0:T(128)S(1)} %multiply_reduce_fusion.1), channel_id=1, replica_groups=mesh['patch'=16,'col'=8] {'patch','col'}, use_global_device_ids=true, to_apply=%region_24.0 | all-reduce | flops 16 | bytes 128 | tf_op jit(solution)/shard_map/psum | solution.py:106
  874.5 64.0 %psum.95 = f32[16]{0:T(128)S(1)} all-reduce(f32[16]{0:T(128)S(1)} %multiply_reduce_fusion), channel_id=1, replica_groups=mesh['patch'=16,'col'=8] {'patch','col'}, use_global_device_ids=true, to_apply=%region_26.0 | all-reduce | flops 16 | bytes 128 | tf_op jit(solution)/shard_map/psum | solution.py:109
  939.2 3.1 custom-call.15
  942.6 3.0 custom-call.17
  946.0 4.8 collective-permute-start.13
  950.8 14.3 %all_gather.27 = f32[32,16,128]{2,1,0:T(8,128)S(1)} all-gather(f32[4,16,128]{2,1,0:T(8,128)S(1)} %add_add_fusion), channel_id=1, replica_groups=mesh['patch'=16,'col'=8] {'col'}, dimensions={0}, use_global_device_ids=true | all-gather | bytes 294912 | tf_op jit(solution)/shard_map/all_gather | solution.py:61
  965.8 8.0 fusion.3
  (99 shorter events, 8.5 us)
Async XLA Ops:
  0.6 95.9 %copy-start = (f32[4,128,128]{2,1,0:T(8,128)S(1)}, f32[4,128,128]{2,1,0:T(8,128)}, u32[]{:S(2)}) copy-start(f32[4,128,128]{2,1,0:T(8,128)} %param.28) | copy-start | bytes 786436
  0.6 115.9 %copy-start.1 = (f32[4,16,128]{2,1,0:T(8,128)S(1)}, f32[4,16,128]{2,1,0:T(8,128)}, u32[]{:S(2)}) copy-start(f32[4,16,128]{2,1,0:T(8,128)} %param.24) | copy-start | bytes 98308
  0.7 115.9 %copy-start.6 = (f32[4,128]{1,0:T(4,128)S(1)}, f32[4,128]{1,0:T(4,128)}, u32[]{:S(2)}) copy-start(f32[4,128]{1,0:T(4,128)} %param.26) | copy-start | bytes 6148
  0.7 115.9 %copy-start.5 = (f32[4,128]{1,0:T(4,128)S(1)}, f32[4,128]{1,0:T(4,128)}, u32[]{:S(2)}) copy-start(f32[4,128]{1,0:T(4,128)} %param.29) | copy-start | bytes 6148
  0.7 115.9 %copy-start.4 = (f32[4,128]{1,0:T(4,128)S(1)}, f32[4,128]{1,0:T(4,128)}, u32[]{:S(2)}) copy-start(f32[4,128]{1,0:T(4,128)} %param.30) | copy-start | bytes 6148
  0.7 23.3 %collective-permute-start = (f32[4,16,128]{2,1,0:T(8,128)}, f32[4,16,128]{2,1,0:T(8,128)S(1)}, u32[]{:S(2)}, u32[]{:S(2)}) collective-permute-start(f32[4,16,128]{2,1,0:T(8,128)} %param.24), channel_id=1, source_target_pairs={{0,8},{8,16},{16,24},{24,32},{32,40},{40,48},{48,56},{56,64},{64,7... | collective-permute-start | bytes 98312 | tf_op jit(solution)/shard_map/ppermute | solution.py:15
  2.8 21.2 %collective-permute-start.1 = (f32[4,16,128]{2,1,0:T(8,128)}, f32[4,16,128]{2,1,0:T(8,128)S(1)}, u32[]{:S(2)}, u32[]{:S(2)}) collective-permute-start(f32[4,16,128]{2,1,0:T(8,128)} %param.24), channel_id=1, source_target_pairs={{0,120},{8,0},{16,8},{24,16},{32,24},{40,32},{48,40},{56,48},{64,5... | collective-permute-start | bytes 98312 | tf_op jit(solution)/shard_map/ppermute | solution.py:15
  97.1 18.7 %collective-permute-start.2 = (f32[4,16,128]{2,1,0:T(8,128)S(1)}, f32[4,16,128]{2,1,0:T(8,128)S(1)}, u32[]{:S(2)}, u32[]{:S(2)}) collective-permute-start(f32[4,16,128]{2,1,0:T(8,128)S(1)} %fusion.43), channel_id=1, source_target_pairs={{0,8},{8,16},{16,24},{24,32},{32,40},{40,48},{48,56},{56,64},{64,7... | collective-permute-start | bytes 98312 | tf_op jit(solution)/shard_map/ppermute | solution.py:15
  97.3 18.4 %collective-permute-start.3 = (f32[4,16,128]{2,1,0:T(8,128)S(1)}, f32[4,16,128]{2,1,0:T(8,128)S(1)}, u32[]{:S(2)}, u32[]{:S(2)}) collective-permute-start(f32[4,16,128]{2,1,0:T(8,128)S(1)} %fusion.43), channel_id=1, source_target_pairs={{0,120},{8,0},{16,8},{24,16},{32,24},{40,32},{48,40},{56,48},{64,5... | collective-permute-start | bytes 98312 | tf_op jit(solution)/shard_map/ppermute | solution.py:15
  251.2 18.6 %collective-permute-start.4 = (f32[4,16,128]{2,1,0:T(8,128)S(1)}, f32[4,16,128]{2,1,0:T(8,128)S(1)}, u32[]{:S(2)}, u32[]{:S(2)}) collective-permute-start(f32[4,16,128]{2,1,0:T(8,128)S(1)} %fusion.44), channel_id=1, source_target_pairs={{0,8},{8,16},{16,24},{24,32},{32,40},{40,48},{48,56},{56,64},{64,7... | collective-permute-start | bytes 98312 | tf_op jit(solution)/shard_map/ppermute | solution.py:15
  252.1 17.7 %collective-permute-start.5 = (f32[4,16,128]{2,1,0:T(8,128)S(1)}, f32[4,16,128]{2,1,0:T(8,128)S(1)}, u32[]{:S(2)}, u32[]{:S(2)}) collective-permute-start(f32[4,16,128]{2,1,0:T(8,128)S(1)} %fusion.44), channel_id=1, source_target_pairs={{0,120},{8,0},{16,8},{24,16},{32,24},{40,32},{48,40},{56,48},{64,5... | collective-permute-start | bytes 98312 | tf_op jit(solution)/shard_map/ppermute | solution.py:15
  269.8 226.9 %copy-start.2 = (f32[4,16,128]{2,1,0:T(8,128)S(1)}, f32[4,16,128]{2,1,0:T(8,128)}, u32[]{:S(2)}) copy-start(f32[4,16,128]{2,1,0:T(8,128)} %param.25) | copy-start | bytes 98308
  476.7 19.3 %collective-permute-start.6 = (f32[4,16,128]{2,1,0:T(8,128)S(1)}, f32[4,16,128]{2,1,0:T(8,128)S(1)}, u32[]{:S(2)}, u32[]{:S(2)}) collective-permute-start(f32[4,16,128]{2,1,0:T(8,128)S(1)} %add_add_fusion.1), channel_id=1, source_target_pairs={{0,8},{8,16},{16,24},{24,32},{32,40},{40,48},{48,56},{56,64},{64,7... | collective-permute-start | bytes 98312 | tf_op jit(solution)/shard_map/ppermute | solution.py:15
  476.7 19.3 %collective-permute-start.7 = (f32[4,16,128]{2,1,0:T(8,128)S(1)}, f32[4,16,128]{2,1,0:T(8,128)S(1)}, u32[]{:S(2)}, u32[]{:S(2)}) collective-permute-start(f32[4,16,128]{2,1,0:T(8,128)S(1)} %add_add_fusion.1), channel_id=1, source_target_pairs={{0,120},{8,0},{16,8},{24,16},{32,24},{40,32},{48,40},{56,48},{64,5... | collective-permute-start | bytes 98312 | tf_op jit(solution)/shard_map/ppermute | solution.py:15
  566.6 18.7 %collective-permute-start.8 = (f32[4,16,128]{2,1,0:T(8,128)S(1)}, f32[4,16,128]{2,1,0:T(8,128)S(1)}, u32[]{:S(2)}, u32[]{:S(2)}) collective-permute-start(f32[4,16,128]{2,1,0:T(8,128)S(1)} %fusion.45), channel_id=1, source_target_pairs={{0,8},{8,16},{16,24},{24,32},{32,40},{40,48},{48,56},{56,64},{64,7... | collective-permute-start | bytes 98312 | tf_op jit(solution)/shard_map/ppermute | solution.py:15
  567.7 17.5 %collective-permute-start.9 = (f32[4,16,128]{2,1,0:T(8,128)S(1)}, f32[4,16,128]{2,1,0:T(8,128)S(1)}, u32[]{:S(2)}, u32[]{:S(2)}) collective-permute-start(f32[4,16,128]{2,1,0:T(8,128)S(1)} %fusion.45), channel_id=1, source_target_pairs={{0,120},{8,0},{16,8},{24,16},{32,24},{40,32},{48,40},{56,48},{64,5... | collective-permute-start | bytes 98312 | tf_op jit(solution)/shard_map/ppermute | solution.py:15
  720.2 18.8 %collective-permute-start.10 = (f32[4,16,128]{2,1,0:T(8,128)S(1)}, f32[4,16,128]{2,1,0:T(8,128)S(1)}, u32[]{:S(2)}, u32[]{:S(2)}) collective-permute-start(f32[4,16,128]{2,1,0:T(8,128)S(1)} %fusion.46), channel_id=1, source_target_pairs={{0,8},{8,16},{16,24},{24,32},{32,40},{40,48},{48,56},{56,64},{64,7... | collective-permute-start | bytes 98312 | tf_op jit(solution)/shard_map/ppermute | solution.py:15
  721.1 17.9 %collective-permute-start.11 = (f32[4,16,128]{2,1,0:T(8,128)S(1)}, f32[4,16,128]{2,1,0:T(8,128)S(1)}, u32[]{:S(2)}, u32[]{:S(2)}) collective-permute-start(f32[4,16,128]{2,1,0:T(8,128)S(1)} %fusion.46), channel_id=1, source_target_pairs={{0,120},{8,0},{16,8},{24,16},{32,24},{40,32},{48,40},{56,48},{64,5... | collective-permute-start | bytes 98312 | tf_op jit(solution)/shard_map/ppermute | solution.py:15
  945.9 27.9 %copy-start.3 = (f32[4,16,128]{2,1,0:T(8,128)}, f32[4,16,128]{2,1,0:T(8,128)S(1)}, u32[]{:S(2)}) copy-start(f32[4,16,128]{2,1,0:T(8,128)S(1)} %add_add_fusion) | copy-start | bytes 98308
  945.9 19.2 %collective-permute-start.12 = (f32[4,16,128]{2,1,0:T(8,128)S(1)}, f32[4,16,128]{2,1,0:T(8,128)S(1)}, u32[]{:S(2)}, u32[]{:S(2)}) collective-permute-start(f32[4,16,128]{2,1,0:T(8,128)S(1)} %add_add_fusion), channel_id=1, source_target_pairs={{0,8},{8,16},{16,24},{24,32},{32,40},{40,48},{48,56},{56,64},{64,7... | collective-permute-start | bytes 98312 | tf_op jit(solution)/shard_map/ppermute | solution.py:15
  946.0 19.1 %collective-permute-start.13 = (f32[4,16,128]{2,1,0:T(8,128)S(1)}, f32[4,16,128]{2,1,0:T(8,128)S(1)}, u32[]{:S(2)}, u32[]{:S(2)}) collective-permute-start(f32[4,16,128]{2,1,0:T(8,128)S(1)} %add_add_fusion), channel_id=1, source_target_pairs={{0,120},{8,0},{16,8},{24,16},{32,24},{40,32},{48,40},{56,48},{64,5... | collective-permute-start | bytes 98312 | tf_op jit(solution)/shard_map/ppermute | solution.py:15
where the time goes:
time: 984 us; the launch traced here: 974 us
  blocking collectives  860 us (87%)
  matrix products  55.7 us (6%)
  starting transfers between devices  34.8 us (4%)
  other arithmetic  16.5 us (2%)
    psum x6, blocking collectives, body(): coeff = lax.psum(column_sum(basis[place], image), ('patch', 'col'))  381 us
    psum x4, blocking collectives, body(): norm = jnp.sqrt(lax.psum(column_sum(image, image), ('patch', 'col')) + EPS)  254 us
    psum x2, blocking collectives, body(): beta = jnp.sqrt(lax.psum(column_sum(start, start), ('patch', 'col')) + EPS)  126 us
    all_gather x7, blocking collectives, near_field(): own_patch = lax.all_gather(field, 'col', axis=0, tiled=True)  99.4 us
    dot_general x7, matrix products, near_field(): jnp.einsum('bkij,bkcj->bci', nearfield, sources * live_mask[:, :, None, N...  52.9 us
    ppermute x14, starting transfers between devices, from_behind(): lax.ppermute(array, axis, [(i, (i + by) % size) for i in range(size)])  34.8 us
  transfers between devices with their start and end apart: 14, of which 0 were waited for; matrix products, arithmetic and copies ran while one was open for 0% of the time, Pallas kernels for 0%

commit v1 on v0

--- a/solution.py
+++ b/solution.py
@@ -8,6 +8,28 @@
 ALPHA = 0.6
 BETA = 0.4
 EPS = 1e-06
+
+
+def joined_along(pieces, dim):
+    pieces = jnp.moveaxis(pieces, 0, dim)
+    lengths = pieces.shape
+    return pieces.reshape(*lengths[:dim], lengths[dim] * lengths[dim + 1], *lengths[dim + 2 :])
+
+
+def ring_gather(x, axis, dim):
+    peers = lax.axis_size(axis)
+    pairs = [(i, (i + 1) % peers) for i in range(peers)]
+    back = [(b, a) for a, b in pairs]
+    lower, upper = ([], [])
+    for step in range(peers - 1):
+        if step % 2 == 0:
+            lower.append(lax.ppermute(lower[-1] if lower else x, axis, pairs))
+        else:
+            upper.append(lax.ppermute(upper[-1] if upper else x, axis, back))
+    blocks = jnp.stack([*lower[::-1], x, *upper])
+    shift = lax.axis_index(axis) - len(lower)
+    blocks = blocks[(jnp.arange(peers) - shift) % peers]
+    return joined_along(blocks, dim)
 
 
 def from_behind(array, axis, by):
@@ -58,7 +80,7 @@
     conduct = conductance[:, None, :]
 
     def near_field(field):
-        own_patch = lax.all_gather(field, "col", axis=0, tiled=True)
+        own_patch = ring_gather(field, "col", 0)
         before = from_behind(field, "patch", 1)
         following = from_behind(field, "patch", -1)
         stacked = jnp.concatenate([own_patch, before, following], axis=0)

time: 984 us -> 1020 us (1.037)
  starting transfers between devices: 34.8 us -> 121 us
  blocking collectives: 860 us -> 782 us
  waiting for transfers between devices: 0.04 us -> 22.6 us
    all_gather x7 -> x0, blocking collectives: 99.4 us -> none  [near_field(): own_patch = lax.all_gather(field, 'col', axis=0, tiled=True)]
    ppermute x0 -> x49, starting transfers between devices: none -> 86.9 us  [the longest x21 43.9 us: ring_gather(): upper.append(lax.ppermute(upper[-1] if upper else x, axis, back))]
    ppermute x0 -> x49, waiting for transfers between devices: none -> 22.6 us  [the longest x28 17.7 us: ring_gather(): lower.append(lax.ppermute(lower[-1] if lower else x, axis, pairs))]
    psum x6, blocking collectives: 381 us -> 396 us  [body(): coeff = lax.psum(column_sum(basis[place], image), ('patch', 'col'))]
  transfers between devices with their start and end apart: 14 -> 63, of which waited for: 0 -> 28; matrix products, arithmetic and copies ran while one was open for 0% -> 1% of each run, Pallas kernels for 0% -> 0%
where the time goes in v1:
time: 1020 us; the launch traced here: 1010 us
  blocking collectives  782 us (77%)
  starting transfers between devices  121 us (12%)
  matrix products  55.7 us (5%)
  waiting for transfers between devices  22.6 us (2%)
  other arithmetic  16.5 us (2%)
  local copies, waits for them, and re-layouts  11.1 us (1%)
    psum x6, blocking collectives, body(): coeff = lax.psum(column_sum(basis[place], image), ('patch', 'col'))  396 us
    psum x4, blocking collectives, body(): norm = jnp.sqrt(lax.psum(column_sum(image, image), ('patch', 'col')) + EPS)  252 us
    psum x2, blocking collectives, body(): beta = jnp.sqrt(lax.psum(column_sum(start, start), ('patch', 'col')) + EPS)  135 us
    dot_general x7, matrix products, near_field(): jnp.einsum('bkij,bkcj->bci', nearfield, sources * live_mask[:, :, None, N...  52.9 us
    ppermute x21, starting transfers between devices, ring_gather(): upper.append(lax.ppermute(upper[-1] if upper else x, axis, back))  43.9 us
    ppermute x28, starting transfers between devices, ring_gather(): lower.append(lax.ppermute(lower[-1] if lower else x, axis, pairs))  43 us
    ppermute x14, starting transfers between devices, from_behind(): lax.ppermute(array, axis, [(i, (i + by) % size) for i in range(size)])  34.1 us
  transfers between devices with their start and end apart: 63, of which 28 were waited for; matrix products, arithmetic and copies ran while one was open for 1% of the time, Pallas kernels for 0%

profile of v1, /device:TPU:1, one launch (start us, length us, event | category | flops | bytes accessed | tf_op | source)
XLA Modules:
  0.0 1010.6 jit_solution(12729677427613916824)
XLA Ops:
  0.6 3.0 collective-permute-start
  4.9 3.7 collective-permute-start.8
  14.0 2.3 collective-permute-start.2
  19.8 2.7 collective-permute-start.6
  25.3 7.6 multiply_reduce_fusion.11
  32.8 67.3 %psum.84 = f32[16]{0:T(128)S(1)} all-reduce(f32[16]{0:T(128)S(1)} %get-tuple-element.61), channel_id=1, replica_groups=mesh['patch'=16,'col'=8] {'patch','col'}, use_global_device_ids=true, to_apply=%region_2.3 | all-reduce | flops 16 | bytes 128 | tf_op jit(solution)/shard_map/psum | solution.py:113
  102.7 2.3 collective-permute-start.10
  111.7 4.8 collective-permute-start.17
  116.5 3.8 collective-permute-start.15
  122.5 7.5 multiply_reduce_fusion.10
  130.0 67.3 %psum.85 = f32[16]{0:T(128)S(1)} all-reduce(f32[16]{0:T(128)S(1)} %get-tuple-element.63), channel_id=1, replica_groups=mesh['patch'=16,'col'=8] {'patch','col'}, use_global_device_ids=true, to_apply=%region_4.5 | all-reduce | flops 16 | bytes 128 | tf_op jit(solution)/shard_map/psum | solution.py:128
  197.5 62.6 %psum.86 = f32[16]{0:T(128)S(1)} all-reduce(f32[16]{0:T(128)S(1)} %multiply_reduce_fusion.9), channel_id=1, replica_groups=mesh['patch'=16,'col'=8] {'patch','col'}, use_global_device_ids=true, to_apply=%region_6.7 | all-reduce | flops 16 | bytes 128 | tf_op jit(solution)/shard_map/psum | solution.py:131
  263.3 2.3 collective-permute-start.19
  266.7 2.3 collective-permute-start.20
  272.8 4.8 collective-permute-start.26
  277.6 3.2 collective-permute-start.24
  283.0 7.5 multiply_reduce_fusion.8
  290.5 67.2 %psum.87 = f32[16]{0:T(128)S(1)} all-reduce(f32[16]{0:T(128)S(1)} %get-tuple-element.65), channel_id=1, replica_groups=mesh['patch'=16,'col'=8] {'patch','col'}, use_global_device_ids=true, to_apply=%region_8.9 | all-reduce | flops 16 | bytes 128 | tf_op jit(solution)/shard_map/psum | solution.py:128
  357.8 63.5 %psum.88 = f32[16]{0:T(128)S(1)} all-reduce(f32[16]{0:T(128)S(1)} %multiply_reduce_fusion.7), channel_id=1, replica_groups=mesh['patch'=16,'col'=8] {'patch','col'}, use_global_device_ids=true, to_apply=%region_10.11 | all-reduce | flops 16 | bytes 128 | tf_op jit(solution)/shard_map/psum | solution.py:128
  421.6 62.7 %psum.89 = f32[16]{0:T(128)S(1)} all-reduce(f32[16]{0:T(128)S(1)} %multiply_reduce_fusion.6), channel_id=1, replica_groups=mesh['patch'=16,'col'=8] {'patch','col'}, use_global_device_ids=true, to_apply=%region_12.13 | all-reduce | flops 16 | bytes 128 | tf_op jit(solution)/shard_map/psum | solution.py:131
  484.9 3.1 custom-call.12
  488.3 3.0 custom-call.14
  494.2 2.3 collective-permute-start.28
  497.5 2.3 collective-permute-start.29
  503.2 4.8 collective-permute-start.35
  508.0 3.3 collective-permute-start.33
  513.4 7.5 multiply_reduce_fusion.5
  520.9 67.4 %psum.90 = f32[16]{0:T(128)S(1)} all-reduce(f32[16]{0:T(128)S(1)} %get-tuple-element.67), channel_id=1, replica_groups=mesh['patch'=16,'col'=8] {'patch','col'}, use_global_device_ids=true, to_apply=%region_16.20 | all-reduce | flops 16 | bytes 128 | tf_op jit(solution)/shard_map/psum | solution.py:113
  596.0 2.8 collective-permute-start.41
  599.8 4.6 collective-permute-start.44
  604.3 4.4 collective-permute-start.42
  610.9 7.5 multiply_reduce_fusion.4
  618.4 67.3 %psum.91 = f32[16]{0:T(128)S(1)} all-reduce(f32[16]{0:T(128)S(1)} %get-tuple-element.69), channel_id=1, replica_groups=mesh['patch'=16,'col'=8] {'patch','col'}, use_global_device_ids=true, to_apply=%region_18.22 | all-reduce | flops 16 | bytes 128 | tf_op jit(solution)/shard_map/psum | solution.py:128
  685.9 62.5 %psum.92 = f32[16]{0:T(128)S(1)} all-reduce(f32[16]{0:T(128)S(1)} %multiply_reduce_fusion.3), channel_id=1, replica_groups=mesh['patch'=16,'col'=8] {'patch','col'}, use_global_device_ids=true, to_apply=%region_20.24 | all-reduce | flops 16 | bytes 128 | tf_op jit(solution)/shard_map/psum | solution.py:131
  751.6 2.3 collective-permute-start.46
  755.0 2.3 collective-permute-start.47
  760.6 4.8 collective-permute-start.53
  765.4 3.2 collective-permute-start.51
  770.8 7.5 multiply_reduce_fusion.2
  778.3 67.5 %psum.93 = f32[16]{0:T(128)S(1)} all-reduce(f32[16]{0:T(128)S(1)} %get-tuple-element.71), channel_id=1, replica_groups=mesh['patch'=16,'col'=8] {'patch','col'}, use_global_device_ids=true, to_apply=%region_22.26 | all-reduce | flops 16 | bytes 128 | tf_op jit(solution)/shard_map/psum | solution.py:128
  846.0 62.9 %psum.94 = f32[16]{0:T(128)S(1)} all-reduce(f32[16]{0:T(128)S(1)} %multiply_reduce_fusion.1), channel_id=1, replica_groups=mesh['patch'=16,'col'=8] {'patch','col'}, use_global_device_ids=true, to_apply=%region_24.28 | all-reduce | flops 16 | bytes 128 | tf_op jit(solution)/shard_map/psum | solution.py:128
  909.1 63.8 %psum.95 = f32[16]{0:T(128)S(1)} all-reduce(f32[16]{0:T(128)S(1)} %multiply_reduce_fusion), channel_id=1, replica_groups=mesh['patch'=16,'col'=8] {'patch','col'}, use_global_device_ids=true, to_apply=%region_26.30 | all-reduce | flops 16 | bytes 128 | tf_op jit(solution)/shard_map/psum | solution.py:131
  973.5 3.1 custom-call.15
  976.9 3.0 custom-call.17
  986.9 3.3 collective-permute-start.59
  991.1 4.7 collective-permute-start.62
  995.8 4.4 collective-permute-start.60
  1002.4 8.0 fusion.3
  (255 shorter events, 76.9 us)
Async XLA Ops:
  0.6 10.2 %collective-permute-start = (f32[4,16,128]{2,1,0:T(8,128)}, f32[4,16,128]{2,1,0:T(8,128)S(1)}, u32[]{:S(2)}, u32[]{:S(2)}) collective-permute-start(f32[4,16,128]{2,1,0:T(8,128)} %param.24), channel_id=1, source_target_pairs={{0,1},{1,2},{2,3},{3,4},{4,5},{5,6},{6,7},{7,0},{8,9},{9,10},{10,1... | collective-permute-start | bytes 98312 | tf_op jit(solution)/shard_map/ppermute | solution.py:26
  3.7 12.8 %collective-permute-start.4 = (f32[4,16,128]{2,1,0:T(8,128)}, f32[4,16,128]{2,1,0:T(8,128)S(1)}, u32[]{:S(2)}, u32[]{:S(2)}) collective-permute-start(f32[4,16,128]{2,1,0:T(8,128)} %param.24), channel_id=1, source_target_pairs={{1,0},{2,1},{3,2},{4,3},{5,4},{6,5},{7,6},{0,7},{9,8},{10,9},{11,1... | collective-permute-start | bytes 98312 | tf_op jit(solution)/shard_map/ppermute | solution.py:28
  3.7 20.8 %collective-permute-start.7 = (f32[4,16,128]{2,1,0:T(8,128)}, f32[4,16,128]{2,1,0:T(8,128)S(1)}, u32[]{:S(2)}, u32[]{:S(2)}) collective-permute-start(f32[4,16,128]{2,1,0:T(8,128)} %param.24), channel_id=1, source_target_pairs={{0,8},{8,16},{16,24},{24,32},{32,40},{40,48},{48,56},{56,64},{64,7... | collective-permute-start | bytes 98312 | tf_op jit(solution)/shard_map/ppermute | solution.py:37
  4.9 19.6 %collective-permute-start.8 = (f32[4,16,128]{2,1,0:T(8,128)}, f32[4,16,128]{2,1,0:T(8,128)S(1)}, u32[]{:S(2)}, u32[]{:S(2)}) collective-permute-start(f32[4,16,128]{2,1,0:T(8,128)} %param.24), channel_id=1, source_target_pairs={{0,120},{8,0},{16,8},{24,16},{32,24},{40,32},{48,40},{56,48},{64,5... | collective-permute-start | bytes 98312 | tf_op jit(solution)/shard_map/ppermute | solution.py:37
  14.0 4.5 collective-permute-start.2
  18.5 4.6 collective-permute-start.3
  19.8 4.1 collective-permute-start.6
  102.7 3.8 collective-permute-start.10
  105.1 3.3 collective-permute-start.13
  106.5 4.6 collective-permute-start.11
  108.4 8.1 collective-permute-start.14
  111.1 9.2 collective-permute-start.12
  111.7 10.0 collective-permute-start.16
  111.7 10.0 collective-permute-start.17
  116.5 4.6 collective-permute-start.15
  265.7 3.4 collective-permute-start.22
  266.7 4.3 collective-permute-start.20
  269.0 8.6 collective-permute-start.23
  271.0 9.7 collective-permute-start.21
  272.3 9.9 collective-permute-start.25
  272.8 9.4 collective-permute-start.26
  277.6 4.1 collective-permute-start.24
  497.5 4.5 collective-permute-start.29
  499.9 8.1 collective-permute-start.32
  502.0 9.2 collective-permute-start.30
  503.2 9.5 collective-permute-start.34
  503.2 9.5 collective-permute-start.35
  508.0 4.1 collective-permute-start.33
  590.5 4.6 collective-permute-start.37
  595.0 4.6 collective-permute-start.38
  596.0 8.3 collective-permute-start.41
  599.6 9.2 collective-permute-start.39
  599.6 10.6 %collective-permute-start.43 = (f32[4,16,128]{2,1,0:T(8,128)S(1)}, f32[4,16,128]{2,1,0:T(8,128)S(1)}, u32[]{:S(2)}, u32[]{:S(2)}) collective-permute-start(f32[4,16,128]{2,1,0:T(8,128)S(1)} %fusion.47), channel_id=1, source_target_pairs={{0,8},{8,16},{16,24},{24,32},{32,40},{40,48},{48,56},{56,64},{64,7... | collective-permute-start | bytes 98312 | tf_op jit(solution)/shard_map/ppermute | solution.py:37
  599.8 10.4 %collective-permute-start.44 = (f32[4,16,128]{2,1,0:T(8,128)S(1)}, f32[4,16,128]{2,1,0:T(8,128)S(1)}, u32[]{:S(2)}, u32[]{:S(2)}) collective-permute-start(f32[4,16,128]{2,1,0:T(8,128)S(1)} %fusion.47), channel_id=1, source_target_pairs={{0,120},{8,0},{16,8},{24,16},{32,24},{40,32},{48,40},{56,48},{64,5... | collective-permute-start | bytes 98312 | tf_op jit(solution)/shard_map/ppermute | solution.py:37
  604.3 5.3 collective-permute-start.42
  755.0 4.4 collective-permute-start.47
  757.3 8.1 collective-permute-start.50
  759.4 9.2 collective-permute-start.48
  760.6 9.4 collective-permute-start.52
  760.6 9.4 collective-permute-start.53
  765.4 4.1 collective-permute-start.51
  981.9 4.5 collective-permute-start.55
  986.4 4.6 collective-permute-start.56
  986.9 8.8 collective-permute-start.59
  991.0 9.2 collective-permute-start.57
  991.0 10.6 %collective-permute-start.61 = (f32[4,16,128]{2,1,0:T(8,128)S(1)}, f32[4,16,128]{2,1,0:T(8,128)S(1)}, u32[]{:S(2)}, u32[]{:S(2)}) collective-permute-start(f32[4,16,128]{2,1,0:T(8,128)S(1)} %add_add_fusion), channel_id=1, source_target_pairs={{0,8},{8,16},{16,24},{24,32},{32,40},{40,48},{48,56},{56,64},{64,7... | collective-permute-start | bytes 98312 | tf_op jit(solution)/shard_map/ppermute | solution.py:37
  991.1 10.6 %collective-permute-start.62 = (f32[4,16,128]{2,1,0:T(8,128)S(1)}, f32[4,16,128]{2,1,0:T(8,128)S(1)}, u32[]{:S(2)}, u32[]{:S(2)}) collective-permute-start(f32[4,16,128]{2,1,0:T(8,128)S(1)} %add_add_fusion), channel_id=1, source_target_pairs={{0,120},{8,0},{16,8},{24,16},{32,24},{40,32},{48,40},{56,48},{64,5... | collective-permute-start | bytes 98312 | tf_op jit(solution)/shard_map/ppermute | solution.py:37
  995.8 5.3 collective-permute-start.60
  (22 other events, 795.8 us)
